TPU v7x, 256 devices: a whole 4x4x8 slice. The times are simulated.
256 devices in a mesh: ia: 32 (over z, x_lo, core), ja: 4 (over y), ka: 2 (over x_hi).
Axes of the slice: x: 4 (x_hi: 2, x_lo: 2; x = x_hi * 2 + x_lo), y: 4, z: 8, core: 2. Of those that a mesh axis runs over, the one named last changes fastest.
Arguments:
- tensor: float32 [8192, 8, 8192], P('ja', 'ka', 'ia'), may hold values from -6 to 6
- factor_a: float32 [8192, 128], P('ia'), may hold values from -1 to 1
- factor_c: float32 [8, 128], P('ka'), may hold values from -2 to 2
- gram_c: float32 [128, 128], replicated, may hold values from -12 to 24, as said below
Outputs:
- factor_b: float32 [8192, 128], P('ja')
- factor_c_new: float32 [8, 128], P('ka')
Inputs may be any that keep to these rules, and one draw needn't show every extreme that they name: `gram_c`: symmetric positive definite.
All inputs are finite; a program needn't handle non-finite values.
Results may differ from a plain program's by a relative error of at most 0.000071.
Values sent between devices are 32-bit elements; how exact they have to be, the bound alone decides.
No kernel may reach another device: no remote copies, remote signals or barrier semaphores. Data moves between devices by JAX's collectives and lax.ppermute only.
A program may use at most 64 MiB of HBM per device.

v0:
```python
import jax
import jax.numpy as jnp
from jax import lax
from jax.sharding import PartitionSpec as P


def right_solve(rhs, system):
    lower = jnp.linalg.cholesky(system)
    middle = lax.linalg.triangular_solve(lower, rhs, left_side=False, lower=True, transpose_a=True)
    return lax.linalg.triangular_solve(
        lower, middle, left_side=False, lower=True, transpose_a=False
    )


def body(tensor, factor_a, factor_c, gram_c):
    high = lax.Precision.HIGHEST
    mode_two, mode_three, mode_one = tensor.shape
    rank = factor_a.shape[1]
    gram_a = lax.psum(
        jnp.dot(factor_a.T, factor_a, precision=high, preferred_element_type=jnp.float32), "ia"
    )
    system_b = gram_a * gram_c
    count = mode_two // lax.axis_size("ia") * lax.axis_size("ia")
    flat = jnp.dot(
        tensor.reshape(count * mode_three, mode_one),
        factor_a,
        precision=high,
        preferred_element_type=jnp.float32,
    )
    shares = lax.psum_scatter(
        flat.reshape(count, mode_three, rank), "ia", scatter_dimension=0, tiled=True
    )
    local_b = lax.psum(jnp.sum(shares * factor_c[None, :, :], axis=1), "ka")
    rows_b = right_solve(local_b, system_b)
    local_c = jnp.sum(shares * rows_b[:, None, :], axis=0)
    local_gram = jnp.dot(rows_b.T, rows_b, precision=high, preferred_element_type=jnp.float32)
    mttkrp_c, gram_b = lax.psum((local_c, local_gram), ("ia", "ja"))
    factor_b = lax.all_gather(rows_b, "ia", axis=0, tiled=True)
    factor_c_new = right_solve(mttkrp_c, gram_a * gram_b)
    return (factor_b, factor_c_new)


def solution(mesh):
    placed = (P("ja", "ka", "ia"), P("ia", None), P("ka", None), P())
    return jax.shard_map(
        body, mesh=mesh, in_specs=placed, out_specs=(P("ja", None), P("ka", None)), check_vma=False
    )
```

profile of v0, /device:TPU:1, one launch (start us, length us, event | category | flops | bytes accessed | tf_op | source)
XLA Modules:
  0.0 1342.1 jit_solution(12914689093623090301)
XLA Ops:
  7.2 0.0 copy-start
  7.2 0.0 all-reduce.3.cloned.1.call-start
  7.2 0.8 copy-done
  8.1 1.0 fusion.15
  9.1 0.0 all-reduce.3.cloned.1.call-update
  9.1 0.0 copy-start.2
  9.1 0.0 copy-start.3
  9.1 0.0 reduce-scatter.2.cloned.1.call-start
  9.2 11.6 fusion
  20.7 0.0 reduce-scatter.2.cloned.1.call-update
  20.8 0.0 all-reduce.5.cloned.1.call-start
  20.8 0.0 copy-done.2
  20.8 0.1 copy.8
  20.9 186.3 %all-reduce.3.cloned.1.call-done = f32[128,128]{0,1:T(8,128)} async-done(((f32[128,128]{0,1:T(8,128)}), f32[128,128]{0,1:T(8,128)}) %all-reduce.3.cloned.1.call-update) | async-done | bytes 65552 | tf_op jit(solution)/shard_map/psum | solution.py:19
  207.2 0.8 mul.24
  208.1 0.1 copy.9
  208.2 11.7 cholesky.44
  220.0 0.6 compare_reduce_fusion.1
  220.6 0.7 fusion.3
  221.3 9.8 custom-call.12
  231.1 97.8 %reduce-scatter.2.cloned.1.call-done = f32[64,4,128]{2,0,1:T(8,128)} async-done(((f32[2048,4,128]{2,0,1:T(8,128)}), f32[64,4,128]{2,0,1:T(8,128)}) %reduce-scatter.2.cloned.1.call-update) | async-done | bytes 131088 | tf_op jit(solution)/shard_map/reduce_scatter | solution.py:30
  328.9 0.0 copy-done.3
  328.9 0.9 multiply_reduce_fusion.1
  329.9 9.2 psum.28
  339.0 0.2 fusion.12
  339.2 0.2 fusion.10
  339.5 0.0 copy-start.1
  339.5 0.9 fusion.16
  340.4 0.0 all-reduce.5.cloned.1.call-update
  340.4 0.0 all-gather.2.cloned.1.call-start
  340.5 0.0 copy-done.1
  340.5 0.5 all-gather.2.cloned.1.call-update
  341.0 0.9 multiply_reduce_fusion
  341.9 277.2 %psum.30 = f32[4,128]{1,0:T(4,128)S(1)} all-reduce(f32[4,128]{1,0:T(4,128)S(1)} %multiply_reduce_fusion), channel_id=1, replica_groups=mesh['ia'=32,'ja'=4,'ka'=2] {'ia','ja'}, use_global_device_ids=true, to_apply=%region_7.9 | all-reduce | flops 512 | bytes 4096 | tf_op jit(solution)/shard_map/psum | solution.py:37
  619.1 650.4 %all-reduce.5.cloned.1.call-done = f32[128,128]{0,1:T(8,128)} async-done(((f32[128,128]{0,1:T(8,128)}), f32[128,128]{0,1:T(8,128)}) %all-reduce.5.cloned.1.call-update) | async-done | bytes 65552 | tf_op jit(solution)/shard_map/psum | solution.py:37
  1269.6 0.9 mul.27
  1270.4 0.1 copy.11
  1270.6 11.7 cholesky.55
  1282.3 0.6 compare_reduce_fusion
  1282.9 0.7 fusion.4
  1283.6 9.8 custom-call.13
  1293.4 0.2 fusion.7
  1293.6 0.8 fusion.5
  1294.4 38.9 %all-gather.2.cloned.1.call-done = f32[2048,128]{1,0:T(8,128)} async-done(((f32[64,128]{1,0:T(8,128)}), f32[2048,128]{1,0:T(8,128)}) %all-gather.2.cloned.1.call-update) | async-done | bytes 1048592 | tf_op jit(solution)/shard_map/all_gather | solution.py:38
  1333.3 2.3 copy.19
  (4 shorter events, 0.1 us)
Async XLA Ops:
  7.2 0.9 copy-start
  7.2 200.1 %all-reduce.3.cloned.1.call-start = ((), (), s32[]{:S(2)}) async-start(), calls=%async_computation.2 | async-start | bytes 131072 | tf_op jit(solution)/shard_map/psum | solution.py:19
  9.1 11.7 copy-start.2
  9.1 319.8 %copy-start.3 = (f32[4,128]{1,0:T(4,128)S(1)}, f32[4,128]{1,0:T(4,128)}, u32[]{:S(2)}) copy-start(f32[4,128]{1,0:T(4,128)} %param.7) | copy-start | bytes 6148
  9.1 319.8 %reduce-scatter.2.cloned.1.call-start = ((), (), s32[]{:S(2)}) async-start(), calls=%async_computation.1 | async-start | bytes 4325376 | tf_op jit(solution)/shard_map/reduce_scatter | solution.py:30
  20.8 1248.8 %all-reduce.5.cloned.1.call-start = ((), (), s32[]{:S(2)}) async-start(), calls=%async_computation.4 | async-start | bytes 131072 | tf_op jit(solution)/shard_map/psum | solution.py:37
  339.5 1.0 copy-start.1
  340.4 992.9 %all-gather.2.cloned.1.call-start = ((), (), s32[]{:S(2)}) async-start(), calls=%async_computation.3 | async-start | bytes 1081344 | tf_op jit(solution)/shard_map/all_gather | solution.py:38
Sparse Core Ops, SparseCore 0:
  11.2 195.9 all-reduce.2
  209.9 118.9 reduce-scatter.1
  340.5 928.9 all-reduce.4
  1271.3 61.9 all-gather.1
where the time goes:
time: 1340 us
  waiting for transfers between devices  974 us (73%)
  blocking collectives  286 us (21%)
  other arithmetic  49.3 us (4%)
  matrix products  14.9 us (1%)
  between operations  13.9 us (1%)
    psum x1, waiting for transfers between devices, body(): mttkrp_c, gram_b = lax.psum((local_c, local_gram), ('ia', 'ja'))  650 us
    psum x1, blocking collectives, body(): mttkrp_c, gram_b = lax.psum((local_c, local_gram), ('ia', 'ja'))  277 us
    psum x1, waiting for transfers between devices, body(): lax.psum(jnp.dot(factor_a.T, factor_a, precision=high, preferred_element_...  186 us
    reduce_scatter x1, waiting for transfers between devices, body(): lax.psum_scatter(flat.reshape(count, mode_three, rank), 'ia', scatter_dim...  97.8 us
    all_gather x1, waiting for transfers between devices, body(): factor_b = lax.all_gather(rows_b, 'ia', axis=0, tiled=True)  38.9 us
  transfers between devices with their start and end apart: 4, of which 4 were waited for; matrix products, arithmetic and copies ran while one was open for 5% of the time, Pallas kernels for 0%

commit v1 on v0

--- a/solution.py
+++ b/solution.py
@@ -13,6 +13,10 @@
 
 
 def body(tensor, factor_a, factor_c, gram_c):
+
+    def resolve_paths(x0):
+        return lax.psum(lax.psum(x0, "ia"), "ja")
+
     high = lax.Precision.HIGHEST
     mode_two, mode_three, mode_one = tensor.shape
     rank = factor_a.shape[1]
@@ -34,7 +38,7 @@
     rows_b = right_solve(local_b, system_b)
     local_c = jnp.sum(shares * rows_b[:, None, :], axis=0)
     local_gram = jnp.dot(rows_b.T, rows_b, precision=high, preferred_element_type=jnp.float32)
-    mttkrp_c, gram_b = lax.psum((local_c, local_gram), ("ia", "ja"))
+    mttkrp_c, gram_b = resolve_paths((local_c, local_gram))
     factor_b = lax.all_gather(rows_b, "ia", axis=0, tiled=True)
     factor_c_new = right_solve(mttkrp_c, gram_a * gram_b)
     return (factor_b, factor_c_new)

time: 1340 us -> 658 us (0.49)
  waiting for transfers between devices: 974 us -> 504 us
  blocking collectives: 286 us -> 71.7 us
    psum x1 -> x2, waiting for transfers between devices: 650 us -> 194 us  [resolve_paths(): return lax.psum(lax.psum(x0, 'ia'), 'ja')]
    psum x1 -> x2, blocking collectives: 277 us -> 62.5 us  [resolve_paths(): return lax.psum(lax.psum(x0, 'ia'), 'ja')]
    all_gather x1, waiting for transfers between devices: 38.9 us -> 25.3 us  [body(): factor_b = lax.all_gather(rows_b, 'ia', axis=0, tiled=True)]
  transfers between devices with their start and end apart: 4 -> 5, of which waited for: 4 -> 4; matrix products, arithmetic and copies ran while one was open for 5% -> 9% of each run, Pallas kernels for 0% -> 0%
where the time goes in v1:
time: 658 us
  waiting for transfers between devices  504 us (77%)
  blocking collectives  71.7 us (11%)
  other arithmetic  49.3 us (7%)
  matrix products  14.9 us (2%)
  between operations  13.9 us (2%)
    psum x2, waiting for transfers between devices, resolve_paths(): return lax.psum(lax.psum(x0, 'ia'), 'ja')  194 us
    psum x1, waiting for transfers between devices, body(): lax.psum(jnp.dot(factor_a.T, factor_a, precision=high, preferred_element_...  186 us
    reduce_scatter x1, waiting for transfers between devices, body(): lax.psum_scatter(flat.reshape(count, mode_three, rank), 'ia', scatter_dim...  97.8 us
    psum x2, blocking collectives, resolve_paths(): return lax.psum(lax.psum(x0, 'ia'), 'ja')  62.5 us
    all_gather x1, waiting for transfers between devices, body(): factor_b = lax.all_gather(rows_b, 'ia', axis=0, tiled=True)  25.3 us
    another operation x6, other arithmetic, right_solve(): lower = jnp.linalg.cholesky(system)  24.8 us
    another operation x4, other arithmetic, right_solve(): lax.linalg.triangular_solve(lower, rhs, left_side=False, lower=True, tran...  20.9 us
  transfers between devices with their start and end apart: 5, of which 4 were waited for; matrix products, arithmetic and copies ran while one was open for 9% of the time, Pallas kernels for 0%

profile of v1, /device:TPU:1, one launch (start us, length us, event | category | flops | bytes accessed | tf_op | source)
XLA Modules:
  0.0 657.5 jit_solution(6715284974032281165)
XLA Ops:
  7.2 0.0 copy-start
  7.2 0.0 all-reduce.4.cloned.1.call-start
  7.2 0.8 copy-done
  8.1 1.0 fusion.15
  9.1 0.0 all-reduce.4.cloned.1.call-update
  9.1 0.0 copy-start.2
  9.1 0.0 copy-start.3
  9.1 0.0 reduce-scatter.2.cloned.1.call-start
  9.2 11.6 %fusion = f32[2048,4,128]{2,0,1:T(8,128)} fusion(f32[2048,4,256]{2,1,0:T(4,128)} %param.5, f32[256,128]{1,0:T(8,128)S(1)} %copy-done), kind=kOutput, calls=%fused_computation | convolution fusion | flops 3221225472 | bytes 12713984 | tf_op jit(solution)/shard_map/dot_general | solution.py:28
  20.7 0.0 reduce-scatter.2.cloned.1.call-update
  20.8 0.0 all-reduce.6.cloned.1.call-start
  20.8 0.0 copy-done.2
  20.8 0.1 copy.8
  20.9 186.3 %all-reduce.4.cloned.1.call-done = f32[128,128]{0,1:T(8,128)} async-done(((f32[128,128]{0,1:T(8,128)}), f32[128,128]{0,1:T(8,128)}) %all-reduce.4.cloned.1.call-update) | async-done | bytes 65552 | tf_op jit(solution)/shard_map/psum | solution.py:23
  207.2 0.8 mul.24
  208.1 0.1 copy.9
  208.2 11.7 %cholesky.44 = f32[128,128]{1,0:T(8,128)S(1)} custom-call(f32[128,128]{1,0:T(8,128)S(1)} %fusion.14), custom_call_target="Cholesky" | custom-call | tf_op jit(solution)/shard_map/jit(cholesky)/cholesky | solution.py:8
  220.0 0.6 compare_reduce_fusion.1
  220.6 0.7 fusion.3
  221.3 9.8 %custom-call.12 = f32[1,128,128]{1,2,0:T(8,128)S(1)} custom-call(f32[1,128,128]{2,1,0:T(8,128)S(1)} %fusion.3), custom_call_target="InvertDiagBlocksLowerTriangular" | custom-call | tf_op jit(solution)/shard_map/triangular_solve | solution.py:9
  231.1 97.8 %reduce-scatter.2.cloned.1.call-done = f32[64,4,128]{2,0,1:T(8,128)} async-done(((f32[2048,4,128]{2,0,1:T(8,128)}), f32[64,4,128]{2,0,1:T(8,128)}) %reduce-scatter.2.cloned.1.call-update) | async-done | bytes 131088 | tf_op jit(solution)/shard_map/reduce_scatter | solution.py:34
  328.9 0.0 copy-done.3
  328.9 0.9 multiply_reduce_fusion.1
  329.9 9.2 %psum.42 = f32[64,128]{1,0:T(8,128)S(1)} all-reduce(f32[64,128]{1,0:T(8,128)S(1)} %multiply_reduce_fusion.1), channel_id=1, replica_groups=mesh['ia'=32,'ja'=4,'ka'=2] {'ka'}, use_global_device_ids=true, to_apply=%region_2.0 | all-reduce | flops 8192 | bytes 65536 | tf_op jit(solution)/shard_map/psum | solution.py:37
  339.0 0.2 fusion.12
  339.2 0.2 fusion.10
  339.5 0.0 copy-start.1
  339.5 0.9 fusion.16
  340.4 0.0 all-reduce.6.cloned.1.call-update
  340.4 0.0 all-reduce.8.cloned.1.call-start
  340.5 194.0 %all-reduce.6.cloned.1.call-done = f32[128,128]{0,1:T(8,128)} async-done(((f32[128,128]{0,1:T(8,128)}), f32[128,128]{0,1:T(8,128)}) %all-reduce.6.cloned.1.call-update) | async-done | bytes 65552 | tf_op jit(solution)/shard_map/psum | solution.py:18
  534.5 0.0 all-reduce.8.cloned.1.call-update
  534.5 0.0 all-gather.2.cloned.1.call-start
  534.5 0.0 copy-done.1
  534.6 0.5 all-gather.2.cloned.1.call-update
  535.1 0.9 multiply_reduce_fusion
  536.0 54.2 %psum.44 = f32[4,128]{1,0:T(4,128)S(1)} all-reduce(f32[4,128]{1,0:T(4,128)S(1)} %multiply_reduce_fusion), channel_id=1, replica_groups=mesh['ia'=32,'ja'=4,'ka'=2] {'ia'}, use_global_device_ids=true, to_apply=%region_7.0 | all-reduce | flops 512 | bytes 4096 | tf_op jit(solution)/shard_map/psum | solution.py:18
  590.2 8.3 %psum.45 = f32[4,128]{1,0:T(4,128)S(1)} all-reduce(f32[4,128]{1,0:T(4,128)S(1)} %psum.44), channel_id=1, replica_groups=mesh['ia'=32,'ja'=4,'ka'=2] {'ja'}, use_global_device_ids=true, to_apply=%region_8.0 | all-reduce | flops 512 | bytes 4096 | tf_op jit(solution)/shard_map/psum | solution.py:18
  598.6 0.9 mul.27
  599.5 0.1 copy.11
  599.6 11.7 %cholesky.55 = f32[128,128]{1,0:T(8,128)S(1)} custom-call(f32[128,128]{1,0:T(8,128)S(1)} %fusion.9), custom_call_target="Cholesky" | custom-call | tf_op jit(solution)/shard_map/jit(cholesky)/cholesky | solution.py:8
  611.3 0.6 compare_reduce_fusion
  612.0 0.7 fusion.4
  612.6 9.8 %custom-call.13 = f32[1,128,128]{1,2,0:T(8,128)S(1)} custom-call(f32[1,128,128]{2,1,0:T(8,128)S(1)} %fusion.4), custom_call_target="InvertDiagBlocksLowerTriangular" | custom-call | tf_op jit(solution)/shard_map/triangular_solve | solution.py:9
  622.4 0.2 fusion.7
  622.6 0.8 fusion.5
  623.4 25.3 %all-gather.2.cloned.1.call-done = f32[2048,128]{1,0:T(8,128)} async-done(((f32[64,128]{1,0:T(8,128)}), f32[2048,128]{1,0:T(8,128)}) %all-gather.2.cloned.1.call-update) | async-done | bytes 1048592 | tf_op jit(solution)/shard_map/all_gather | solution.py:42
  648.7 2.3 copy.20
  (5 shorter events, 0.1 us)
Async XLA Ops:
  7.2 0.9 copy-start
  7.2 200.1 %all-reduce.4.cloned.1.call-start = ((), (), s32[]{:S(2)}) async-start(), calls=%async_computation.2 | async-start | bytes 131072 | tf_op jit(solution)/shard_map/psum | solution.py:23
  9.1 11.7 %copy-start.2 = (f32[128,128]{1,0:T(8,128)S(1)}, f32[128,128]{1,0:T(8,128)}, u32[]{:S(2)}) copy-start(f32[128,128]{1,0:T(8,128)} %param.8) | copy-start | bytes 196612
  9.1 319.8 %copy-start.3 = (f32[4,128]{1,0:T(4,128)S(1)}, f32[4,128]{1,0:T(4,128)}, u32[]{:S(2)}) copy-start(f32[4,128]{1,0:T(4,128)} %param.7) | copy-start | bytes 6148
  9.1 319.8 %reduce-scatter.2.cloned.1.call-start = ((), (), s32[]{:S(2)}) async-start(), calls=%async_computation.1 | async-start | bytes 4325376 | tf_op jit(solution)/shard_map/reduce_scatter | solution.py:34
  20.8 513.7 %all-reduce.6.cloned.1.call-start = ((), (), s32[]{:S(2)}) async-start(), calls=%async_computation.4 | async-start | bytes 131072 | tf_op jit(solution)/shard_map/psum | solution.py:18
  339.5 195.1 %copy-start.1 = (f32[64,128]{1,0:T(8,128)}, f32[64,128]{1,0:T(8,128)S(1)}, u32[]{:S(2)}) copy-start(f32[64,128]{1,0:T(8,128)S(1)} %fusion.10) | copy-start | bytes 98308
  340.4 258.1 %all-reduce.8.cloned.1.call-start = ((), (), s32[]{:S(2)}) async-start(), calls=%async_computation.5 | async-start | bytes 131072 | tf_op jit(solution)/shard_map/psum | solution.py:18
  534.5 114.2 %all-gather.2.cloned.1.call-start = ((), (), s32[]{:S(2)}) async-start(), calls=%async_computation.3 | async-start | bytes 1081344 | tf_op jit(solution)/shard_map/all_gather | solution.py:42
Sparse Core Ops, SparseCore 0:
  11.2 195.9 all-reduce.3
  209.9 118.9 reduce-scatter.1
  340.5 193.8 all-reduce.5
  536.6 43.4 all-reduce.7
  582.0 66.6 all-gather.1
